TPU v7x, 32 devices: a whole 2x2x4 slice. The times are simulated.
32 devices in a mesh: dp: 8 (over z, y), tp: 4 (over x, core).
Axes of the slice: x: 2, y: 2, z: 4, core: 2. Of those that a mesh axis runs over, the one named last changes fastest.
Arguments:
- attn_partial: bfloat16 [4, 512, 7168], P('tp', 'dp'), may hold values from -3 to 3
- hidden_in: bfloat16 [512, 7168], P('dp', 'tp'), may hold values from -6 to 6
- norm_gain: float32 [7168], replicated, may hold values from 0.5 to 1.5
- expert_ids: int32 [512, 8], P('dp'), may hold values from 0 to 255, all different within a row; in each aligned block of 64 rows (0 to 63, 64 to 127, ...) at most 4 rows name the same one
- route_prob: bfloat16 [512, 8], P('dp'), may hold values from 0.049804688 to 0.3984375
- w_gate: bfloat16 [8, 7168, 1024], P('dp', None, 'tp'), may hold values from -0.0625 to 0.0625
- w_up: bfloat16 [8, 7168, 1024], P('dp', None, 'tp'), may hold values from -0.0625 to 0.0625
- w_down: bfloat16 [8, 1024, 7168], P('dp', 'tp'), may hold values from -0.1875 to 0.1875
Outputs:
- layer_out: bfloat16 [512, 7168], P('dp', 'tp')
- amax_input: float32 [8], P('dp')
- amax_hidden: float32 [8], P('dp')
Inputs may be any that keep to these rules, and one draw needn't show every extreme that they name: `expert_ids`: each token names 8 different experts; within each aligned block of 64 tokens no expert is named by more than 4 tokens.
All inputs are finite; a program needn't handle non-finite values.
Results may differ from a plain program's by a relative error of at most 0.0075.
Values may be sent and summed in bfloat16 or wider, within the bound.
No kernel may reach another device: no remote copies, remote signals or barrier semaphores. Data moves between devices by JAX's collectives and lax.ppermute only.
A program may use at most 64 MiB of HBM per device.

v0:
```python
import jax
import jax.numpy as jnp
from jax import lax
from jax.sharding import PartitionSpec as P

EXPERT_SLOTS = 4
eps = 1e-06


def route_tables(expert_ids, route_prob, experts, capacity):
    matches = expert_ids[:, :, None] == jnp.arange(experts, dtype=jnp.int32)[None, None, :]
    onehot = jnp.sum(matches.astype(jnp.int32), axis=1)
    weight = jnp.sum(
        jnp.where(matches, route_prob[:, :, None].astype(jnp.float32), jnp.float32(0.0)), axis=1
    )
    before = jnp.cumsum(onehot, axis=0) - onehot
    placing = (onehot.T[:, None, :] == 1) & (
        before.T[:, None, :] == jnp.arange(capacity, dtype=jnp.int32)[None, :, None]
    )
    return (onehot, weight, placing)


def on_device(attn_partial, hidden_in, norm_gain, expert_ids, route_prob, w_gate, w_up, w_down):
    experts = lax.axis_size("dp")
    tp_index = lax.axis_index("tp")
    partial_value = attn_partial[0].astype(jnp.float32)
    token_count = partial_value.shape[0]
    columns = hidden_in.shape[1]
    start_col = tp_index * columns
    own_cols = lax.dynamic_slice_in_dim(partial_value, start_col, columns, 1) + hidden_in.astype(
        jnp.float32
    )
    summand = lax.dynamic_update_slice_in_dim(partial_value, own_cols, start_col, 1)
    residual = lax.psum(summand, "tp")
    mean_sq = jnp.mean(residual * residual, axis=1, keepdims=True)
    normed = (residual * lax.rsqrt(mean_sq + eps) * norm_gain).astype(jnp.bfloat16)
    residual_cols = lax.dynamic_slice_in_dim(residual, start_col, columns, 1)
    onehot, weight, placing = route_tables(expert_ids, route_prob, experts, EXPERT_SLOTS)
    selection_mask = placing.reshape(experts * EXPERT_SLOTS, token_count).astype(jnp.bfloat16)
    outgoing = jnp.dot(selection_mask, normed, preferred_element_type=jnp.float32).astype(
        jnp.bfloat16
    )
    piece_width = outgoing.shape[1]
    incoming = lax.all_to_all(
        outgoing.reshape(experts, EXPERT_SLOTS, piece_width),
        "dp",
        split_axis=0,
        concat_axis=0,
        tiled=True,
    )
    expert_slot_rows = incoming.reshape(experts * EXPERT_SLOTS, piece_width)
    gate_val = jnp.dot(expert_slot_rows, w_gate[0], preferred_element_type=jnp.float32)
    up_val = jnp.dot(expert_slot_rows, w_up[0], preferred_element_type=jnp.float32)
    hidden_act = (jax.nn.silu(gate_val) * up_val).astype(jnp.bfloat16)
    partial_out = jnp.dot(hidden_act, w_down[0], preferred_element_type=jnp.float32)
    combine_matrix = (placing.astype(jnp.float32) * weight.T[:, None, :]).reshape(
        experts * EXPERT_SLOTS, token_count
    )
    expert_cols = lax.psum_scatter(
        partial_out.astype(jnp.bfloat16), "tp", scatter_dimension=1, tiled=True
    ).astype(jnp.float32)
    returned = lax.all_to_all(
        expert_cols.reshape(experts, EXPERT_SLOTS, columns).astype(jnp.bfloat16),
        "dp",
        split_axis=0,
        concat_axis=0,
        tiled=True,
    ).astype(jnp.float32)
    moe_out = jnp.dot(
        combine_matrix.T,
        returned.reshape(experts * EXPERT_SLOTS, columns),
        precision=lax.Precision.HIGHEST,
        preferred_element_type=jnp.float32,
    )
    layer_out = (residual_cols + moe_out).astype(jnp.bfloat16)
    hidden_peak = jnp.max(jnp.abs(hidden_act.astype(jnp.float32)))
    input_peak = jnp.max(jnp.abs(expert_slot_rows.astype(jnp.float32)))
    input_peak, hidden_peak = lax.pmax((input_peak, hidden_peak), "tp")
    amax_input = input_peak.reshape(1)
    amax_hidden = hidden_peak.reshape(1)
    return (layer_out, amax_input, amax_hidden)


def solution(mesh):
    placed = (
        P("tp", "dp", None),
        P("dp", "tp"),
        P(),
        P("dp", None),
        P("dp", None),
        P("dp", None, "tp"),
        P("dp", None, "tp"),
        P("dp", "tp", None),
    )
    return jax.shard_map(
        on_device,
        mesh=mesh,
        in_specs=placed,
        out_specs=(P("dp", "tp"), P("dp"), P("dp")),
        check_vma=False,
    )
```

profile of v0, /device:TPU:0, one launch (start us, length us, event | category | flops | bytes accessed | tf_op | source)
XLA Modules:
  0.0 132.3 jit_solution(10730123870915161944)
XLA Ops:
  7.2 2.8 %fusion.27 = (f32[1,64,7168]{2,1,0:T(8,128)}, f32[64,7168]{1,0:T(8,128)S(1)}) fusion(bf16[1,64,7168]{2,1,0:T(8,128)(2,1)} %param.8), kind=kLoop, calls=%fused_computation.38 | loop fusion | flops 458752 | bytes 4587520 | tf_op jit(solution)/shard_map/convert_element_type | solution.py:26
  10.1 1.1 fusion.15
  11.2 1.2 copy-done
  12.5 0.1 copy.26
  12.5 0.1 reduce_window_sum.11
  12.7 0.1 eq.58
  12.8 49.6 %all-reduce.3.cloned.1.call-done = f32[64,7168]{1,0:T(8,128)} async-done(((f32[64,7168]{1,0:T(8,128)}), f32[64,7168]{1,0:T(8,128)}) %all-reduce.3.cloned.1.call-update) | async-done | bytes 1835024 | tf_op jit(solution)/shard_map/psum | solution.py:34
  62.4 1.9 %multiply_reduce_fusion = f32[64]{0:T(128)S(1)} fusion(f32[64,7168]{1,0:T(8,128)} %all-reduce.3.cloned.1.call-done), kind=kLoop, calls=%fused_computation.11 | loop fusion | flops 917440 | bytes 1835264 | tf_op jit(solution)/shard_map/reduce_sum | solution.py:35
  64.3 0.1 copy-done.1
  64.4 0.4 convolution_convert_fusion.1
  64.8 0.2 reshape.44
  65.0 18.3 %all_to_all.10 = bf16[8,4,7168]{2,1,0:T(4,128)(2,1)S(1)} all-to-all(bf16[8,4,7168]{2,1,0:T(4,128)(2,1)S(1)} %reshape.44), channel_id=1, replica_groups=mesh['dp'=8,'tp'=4] {'dp'}, dimensions={0} | all-to-all | bytes 917504 | tf_op jit(solution)/shard_map/all_to_all | solution.py:44
  83.3 0.1 reshape.45
  83.4 2.9 %fusion.3 = f32[32,256]{1,0:T(8,128)S(1)} fusion(bf16[32,7168]{1,0:T(8,128)(2,1)S(1)} %reshape.45, bf16[1,7168,256]{2,1,0:T(8,128)(2,1)} %param.13), kind=kOutput, calls=%fused_computation.5 | convolution fusion | flops 117440512 | bytes 4161536 | tf_op jit(solution)/shard_map/dot_general | solution.py:52
  86.3 0.2 copy-done.2
  86.5 1.3 %abs_reduce_fusion.1 = (f32[]{:T(128)}, bf16[32,256]{1,0:T(8,128)(2,1)S(1)}) fusion(bf16[32,7168]{1,0:T(8,128)(2,1)S(1)} %reshape.45, bf16[1,7168,256]{2,1,0:T(8,128)(2,1)S(1)} %copy-done.2, f32[32,256]{1,0:T(8,128)S(1)} %fusion.3), kind=kOutput, calls=%fused_computation.20 | convolution fusion | flops 117514240 | bytes 4177924 | tf_op jit(solution)/shard_map/dot_general | solution.py:53
  87.9 0.7 copy-done.3
  88.6 1.5 %convolution_convert_fusion = bf16[32,7168]{1,0:T(8,128)(2,1)} fusion(bf16[32,256]{1,0:T(8,128)(2,1)S(1)} %get-tuple-element.8, bf16[1,256,7168]{2,1,0:T(8,128)(2,1)S(1)} %copy-done.3), kind=kOutput, calls=%fused_computation | convolution fusion | flops 117669888 | bytes 4145152 | tf_op jit(solution)/shard_map/dot_general | solution.py:55
  90.1 19.5 %reduce-scatter.2.cloned.1.call-done = bf16[32,1792]{1,0:T(8,128)(2,1)} async-done(((bf16[32,7168]{1,0:T(8,128)(2,1)}), bf16[32,1792]{1,0:T(8,128)(2,1)}) %reduce-scatter.2.cloned.1.call-update) | async-done | bytes 114704 | tf_op jit(solution)/shard_map/reduce_scatter | solution.py:59
  109.7 1.6 %convert_element_type.55 = bf16[8,4,1792]{2,1,0:T(4,128)(2,1)} reshape(bf16[32,1792]{1,0:T(8,128)(2,1)} %reduce-scatter.2.cloned.1.call-done) | data formatting | bytes 229376 | tf_op jit(solution)/shard_map/convert_element_type | solution.py:63
  111.2 5.5 %all-to-all-start.1 = ((bf16[8,4,1792]{2,1,0:T(4,128)(2,1)}), bf16[8,4,1792]{2,1,0:T(4,128)(2,1)S(1)}, u32[]{:S(2)}, u32[]{:S(2)}) async-start(bf16[8,4,1792]{2,1,0:T(4,128)(2,1)} %convert_element_type.55), calls=%async_computation.2 | async-start | bytes 229376 | tf_op jit(solution)/shard_map/all_to_all | solution.py:62
  116.7 1.1 abs_reduce_fusion
  117.8 6.6 %all-reduce = (f32[1]{0:T(128)}, f32[1]{0:T(128)}) all-reduce(f32[1]{0:T(128)} %bitcast.11, f32[1]{0:T(128)} %bitcast.12), channel_id=1, replica_groups=mesh['dp'=8,'tp'=4] {'tp'}, use_global_device_ids=true, to_apply=%region_7.8 | all-reduce | flops 2 | bytes 16 | tf_op jit(solution)/shard_map/pmax | solution.py:78
  124.4 1.1 fusion.6
  (27 shorter events, 0.3 us)
Async XLA Ops:
  7.2 55.2 %all-reduce.3.cloned.1.call-start = ((), (), s32[]{:S(2)}) async-start(), calls=%async_computation.3 | async-start | bytes 3670016 | tf_op jit(solution)/shard_map/psum | solution.py:34
  7.2 2.8 %copy-start.4 = (bf16[64,1792]{1,0:T(8,128)(2,1)S(1)}, bf16[64,1792]{1,0:T(8,128)(2,1)}, u32[]{:S(2)}) copy-start(bf16[64,1792]{1,0:T(8,128)(2,1)} %param.9) | copy-start | bytes 688132
  10.1 2.4 %copy-start.6 = (s32[64,8]{0,1:T(8,128)S(1)}, s32[64,8]{0,1:T(8,128)}, u32[]{:S(2)}) copy-start(s32[64,8]{0,1:T(8,128)} %param.11) | copy-start | bytes 6148
  11.1 1.2 copy-start
  11.1 53.1 %copy-start.5 = (f32[7168]{0:T(1024)S(1)}, f32[7168]{0:T(1024)}, u32[]{:S(2)}) copy-start(f32[7168]{0:T(1024)} %param.10) | copy-start | bytes 86020
  12.4 97.3 %reduce-scatter.2.cloned.1.call-start = ((), (), s32[]{:S(2)}) async-start(), calls=%async_computation.4 | async-start | bytes 573440 | tf_op jit(solution)/shard_map/reduce_scatter | solution.py:59
  62.4 2.1 %copy-start.1 = (f32[64,7168]{1,0:T(8,128)S(1)}, f32[64,7168]{1,0:T(8,128)}, u32[]{:S(2)}) copy-start(f32[64,7168]{1,0:T(8,128)} %all-reduce.3.cloned.1.call-done) | copy-start | bytes 5505028
  83.4 3.1 %copy-start.2 = (bf16[1,7168,256]{2,1,0:T(8,128)(2,1)S(1)}, bf16[1,7168,256]{2,1,0:T(8,128)(2,1)}, u32[]{:S(2)}) copy-start(bf16[1,7168,256]{2,1,0:T(8,128)(2,1)} %param.14) | copy-start | bytes 11010052
  86.5 2.0 %copy-start.3 = (bf16[1,256,7168]{2,1,0:T(8,128)(2,1)S(1)}, bf16[1,256,7168]{2,1,0:T(8,128)(2,1)}, u32[]{:S(2)}) copy-start(bf16[1,256,7168]{2,1,0:T(8,128)(2,1)} %param.15) | copy-start | bytes 11010052
  88.6 1.5 %copy-start.7 = (bf16[64,8]{0,1:T(8,128)(2,1)S(1)}, bf16[64,8]{0,1:T(8,128)(2,1)}, u32[]{:S(2)}) copy-start(bf16[64,8]{0,1:T(8,128)(2,1)} %param.12) | copy-start | bytes 3076
  111.2 13.2 %all-to-all-start.1 = ((bf16[8,4,1792]{2,1,0:T(4,128)(2,1)}), bf16[8,4,1792]{2,1,0:T(4,128)(2,1)S(1)}, u32[]{:S(2)}, u32[]{:S(2)}) async-start(bf16[8,4,1792]{2,1,0:T(4,128)(2,1)} %convert_element_type.55), calls=%async_computation.2 | async-start | bytes 229376 | tf_op jit(solution)/shard_map/all_to_all | solution.py:62
Sparse Core Ops, SparseCore 0:
  12.5 49.8 all-reduce.2
  90.2 19.3 reduce-scatter.1
where the time goes:
time: 133 us; the launch traced here: 132 us
  waiting for transfers between devices  69.1 us (52%)
  blocking collectives  24.9 us (19%)
  between operations  14.2 us (11%)
  matrix products  7.23 us (5%)
  other arithmetic  6.96 us (5%)
  starting transfers between devices  5.58 us (4%)
  local copies, waits for them, and re-layouts  4.39 us (3%)
    psum x1, waiting for transfers between devices, on_device(): residual = lax.psum(summand, 'tp')  49.6 us
    reduce_scatter x1, waiting for transfers between devices, on_device(): lax.psum_scatter(partial_out.astype(jnp.bfloat16), 'tp', scatter_dimensio...  19.5 us
    all_to_all x1, blocking collectives, on_device(): lax.all_to_all(outgoing.reshape(experts, EXPERT_SLOTS, piece_width), 'dp'...  18.3 us
    pmax x1, blocking collectives, on_device(): input_peak, hidden_peak = lax.pmax((input_peak, hidden_peak), 'tp')  6.59 us
    all_to_all x1, starting transfers between devices, on_device(): lax.all_to_all(expert_cols.reshape(experts, EXPERT_SLOTS, columns).astype...  5.5 us
    dot_general x1, matrix products, on_device(): jnp.dot(expert_slot_rows, w_gate[0], preferred_element_type=jnp.float32)  2.92 us
    convert_element_type x1, other arithmetic, on_device(): partial_value = attn_partial[0].astype(jnp.float32)  2.83 us
  transfers between devices with their start and end apart: 3, of which 2 were waited for; matrix products, arithmetic and copies ran while one was open for 1% of the time, Pallas kernels for 0%

commit v1 on v0

--- a/solution.py
+++ b/solution.py
@@ -1,3 +1,4 @@
+import functools
 import jax
 import jax.numpy as jnp
 from jax import lax
@@ -5,6 +6,15 @@
 
 EXPERT_SLOTS = 4
 eps = 1e-06
+
+
+def touch_views(my_tile, lane_axis):
+    top = lax.all_gather(my_tile, axis_name=lane_axis)
+    all_rows = jnp.sum(top, axis=0)
+    return all_rows
+
+
+search_ratios_all = functools.partial(touch_views, lane_axis="tp")
 
 
 def route_tables(expert_ids, route_prob, experts, capacity):
@@ -31,7 +41,7 @@
         jnp.float32
     )
     summand = lax.dynamic_update_slice_in_dim(partial_value, own_cols, start_col, 1)
-    residual = lax.psum(summand, "tp")
+    residual = search_ratios_all(summand)
     mean_sq = jnp.mean(residual * residual, axis=1, keepdims=True)
     normed = (residual * lax.rsqrt(mean_sq + eps) * norm_gain).astype(jnp.bfloat16)
     residual_cols = lax.dynamic_slice_in_dim(residual, start_col, columns, 1)

time: 133 us -> 138 us (1.038)
  waiting for transfers between devices: 69.1 us -> 74.1 us
    all_gather x0 -> x1, waiting for transfers between devices: none -> 54.8 us  [touch_views(): top = lax.all_gather(my_tile, axis_name=lane_axis)]
    psum x1 -> x0, waiting for transfers between devices: 49.6 us -> none  [on_device(): residual = lax.psum(summand, 'tp')]
    reduce_sum x0 -> x1, other arithmetic: none -> 3.7 us  [touch_views(): all_rows = jnp.sum(top, axis=0)]
    reduce_sum x1, other arithmetic: 1.85 us -> 0.25 us  [on_device(): mean_sq = jnp.mean(residual * residual, axis=1, keepdims=True)]
    convert_element_type x1, other arithmetic: 2.83 us -> 1.34 us  [on_device(): partial_value = attn_partial[0].astype(jnp.float32)]
where the time goes in v1:
time: 138 us
  waiting for transfers between devices  74.1 us (54%)
  blocking collectives  25.5 us (18%)
  between operations  14.2 us (10%)
  matrix products  7.23 us (5%)
  other arithmetic  6.55 us (5%)
  starting transfers between devices  5.6 us (4%)
  local copies, waits for them, and re-layouts  4.85 us (4%)
    all_gather x1, waiting for transfers between devices, touch_views(): top = lax.all_gather(my_tile, axis_name=lane_axis)  54.8 us
    reduce_scatter x1, waiting for transfers between devices, on_device(): lax.psum_scatter(partial_out.astype(jnp.bfloat16), 'tp', scatter_dimensio...  19.3 us
    all_to_all x1, blocking collectives, on_device(): lax.all_to_all(outgoing.reshape(experts, EXPERT_SLOTS, piece_width), 'dp'...  18.9 us
    pmax x1, blocking collectives, on_device(): input_peak, hidden_peak = lax.pmax((input_peak, hidden_peak), 'tp')  6.58 us
    all_to_all x1, starting transfers between devices, on_device(): lax.all_to_all(expert_cols.reshape(experts, EXPERT_SLOTS, columns).astype...  5.52 us
    reduce_sum x1, other arithmetic, touch_views(): all_rows = jnp.sum(top, axis=0)  3.7 us
    dot_general x1, matrix products, on_device(): jnp.dot(expert_slot_rows, w_gate[0], preferred_element_type=jnp.float32)  2.92 us
  transfers between devices with their start and end apart: 3, of which 2 were waited for; matrix products, arithmetic and copies ran while one was open for 1% of the time, Pallas kernels for 0%

profile of v1, /device:TPU:0, one launch (start us, length us, event | category | flops | bytes accessed | tf_op | source)
XLA Modules:
  0.0 138.1 jit_solution(9590424284655803030)
XLA Ops:
  7.2 1.3 convert_element_type.45
  8.7 1.3 copy-done
  10.1 0.1 copy.26
  10.2 0.1 reduce_window_sum.11
  10.4 0.1 eq.58
  10.5 54.8 %all-gather.2.cloned.1.call-done = f32[4,64,7168]{2,1,0:T(8,128)} async-done(((f32[1,64,7168]{2,1,0:T(8,128)}), f32[4,64,7168]{2,1,0:T(8,128)}) %all-gather.2.cloned.1.call-update) | async-done | bytes 7340048 | tf_op jit(solution)/shard_map/all_gather | solution.py:12
  65.2 3.7 %reduce_sum.36 = f32[64,7168]{1,0:T(8,128)S(1)} reduce(f32[4,64,7168]{2,1,0:T(8,128)} %all-gather.2.cloned.1.call-done, f32[]{:T(128)} %constant.24.clone.1), dimensions={0}, to_apply=%region_0.0 | reduce | flops 1376256 | bytes 9175044 | tf_op jit(solution)/shard_map/reduce_sum | solution.py:13
  68.9 0.2 multiply_reduce_fusion
  69.2 0.5 copy-done.4
  69.7 0.4 convolution_convert_fusion.1
  70.1 0.2 reshape.46
  70.2 18.9 %all_to_all.10 = bf16[8,4,7168]{2,1,0:T(4,128)(2,1)S(1)} all-to-all(bf16[8,4,7168]{2,1,0:T(4,128)(2,1)S(1)} %reshape.46), channel_id=1, replica_groups=mesh['dp'=8,'tp'=4] {'dp'}, dimensions={0} | all-to-all | bytes 917504 | tf_op jit(solution)/shard_map/all_to_all | solution.py:54
  89.2 0.1 reshape.47
  89.3 2.9 %fusion.3 = f32[32,256]{1,0:T(8,128)S(1)} fusion(bf16[32,7168]{1,0:T(8,128)(2,1)S(1)} %reshape.47, bf16[1,7168,256]{2,1,0:T(8,128)(2,1)} %param.13), kind=kOutput, calls=%fused_computation.5 | convolution fusion | flops 117440512 | bytes 4161536 | tf_op jit(solution)/shard_map/dot_general | solution.py:62
  92.2 0.2 copy-done.1
  92.4 1.3 abs_reduce_fusion.1
  93.7 0.7 copy-done.2
  94.5 1.5 %convolution_convert_fusion = bf16[32,7168]{1,0:T(8,128)(2,1)} fusion(bf16[32,256]{1,0:T(8,128)(2,1)S(1)} %get-tuple-element.6, bf16[1,256,7168]{2,1,0:T(8,128)(2,1)S(1)} %copy-done.2), kind=kOutput, calls=%fused_computation | convolution fusion | flops 117669888 | bytes 4145152 | tf_op jit(solution)/shard_map/dot_general | solution.py:65
  96.0 19.3 %reduce-scatter.2.cloned.1.call-done = bf16[32,1792]{1,0:T(8,128)(2,1)} async-done(((bf16[32,7168]{1,0:T(8,128)(2,1)}), bf16[32,1792]{1,0:T(8,128)(2,1)}) %reduce-scatter.2.cloned.1.call-update) | async-done | bytes 114704 | tf_op jit(solution)/shard_map/reduce_scatter | solution.py:69
  115.3 1.6 %convert_element_type.53 = bf16[8,4,1792]{2,1,0:T(4,128)(2,1)} reshape(bf16[32,1792]{1,0:T(8,128)(2,1)} %reduce-scatter.2.cloned.1.call-done) | data formatting | bytes 229376 | tf_op jit(solution)/shard_map/convert_element_type | solution.py:73
  116.9 5.5 %all-to-all-start.1 = ((bf16[8,4,1792]{2,1,0:T(4,128)(2,1)}), bf16[8,4,1792]{2,1,0:T(4,128)(2,1)S(1)}, u32[]{:S(2)}, u32[]{:S(2)}) async-start(bf16[8,4,1792]{2,1,0:T(4,128)(2,1)} %convert_element_type.53), calls=%async_computation.2 | async-start | bytes 229376 | tf_op jit(solution)/shard_map/all_to_all | solution.py:72
  122.5 1.1 abs_reduce_fusion
  123.5 6.6 %all-reduce = (f32[1]{0:T(128)}, f32[1]{0:T(128)}) all-reduce(f32[1]{0:T(128)} %bitcast.11, f32[1]{0:T(128)} %bitcast.12), channel_id=1, replica_groups=mesh['dp'=8,'tp'=4] {'tp'}, use_global_device_ids=true, to_apply=%region_7.8 | all-reduce | flops 2 | bytes 16 | tf_op jit(solution)/shard_map/pmax | solution.py:88
  130.1 1.1 fusion.6
  (27 shorter events, 0.4 us)
Async XLA Ops:
  7.2 58.1 %all-gather.2.cloned.1.call-start = ((), (), s32[]{:S(2)}) async-start(), calls=%async_computation.3 | async-start | bytes 9175040 | tf_op jit(solution)/shard_map/all_gather | solution.py:12
  7.2 1.4 %copy-start.3 = (bf16[64,1792]{1,0:T(8,128)(2,1)S(1)}, bf16[64,1792]{1,0:T(8,128)(2,1)}, u32[]{:S(2)}) copy-start(bf16[64,1792]{1,0:T(8,128)(2,1)} %param.9) | copy-start | bytes 688132
  8.6 1.5 %copy-start.5 = (s32[64,8]{0,1:T(8,128)S(1)}, s32[64,8]{0,1:T(8,128)}, u32[]{:S(2)}) copy-start(s32[64,8]{0,1:T(8,128)} %param.11) | copy-start | bytes 6148
  8.7 1.3 copy-start
  10.0 105.3 %reduce-scatter.2.cloned.1.call-start = ((), (), s32[]{:S(2)}) async-start(), calls=%async_computation.4 | async-start | bytes 573440 | tf_op jit(solution)/shard_map/reduce_scatter | solution.py:69
  68.9 0.8 copy-start.4
  89.3 3.1 %copy-start.1 = (bf16[1,7168,256]{2,1,0:T(8,128)(2,1)S(1)}, bf16[1,7168,256]{2,1,0:T(8,128)(2,1)}, u32[]{:S(2)}) copy-start(bf16[1,7168,256]{2,1,0:T(8,128)(2,1)} %param.14) | copy-start | bytes 11010052
  92.4 2.0 %copy-start.2 = (bf16[1,256,7168]{2,1,0:T(8,128)(2,1)S(1)}, bf16[1,256,7168]{2,1,0:T(8,128)(2,1)}, u32[]{:S(2)}) copy-start(bf16[1,256,7168]{2,1,0:T(8,128)(2,1)} %param.15) | copy-start | bytes 11010052
  94.5 1.5 %copy-start.6 = (bf16[64,8]{0,1:T(8,128)(2,1)S(1)}, bf16[64,8]{0,1:T(8,128)(2,1)}, u32[]{:S(2)}) copy-start(bf16[64,8]{0,1:T(8,128)(2,1)} %param.12) | copy-start | bytes 3076
  116.9 13.2 %all-to-all-start.1 = ((bf16[8,4,1792]{2,1,0:T(4,128)(2,1)}), bf16[8,4,1792]{2,1,0:T(4,128)(2,1)S(1)}, u32[]{:S(2)}, u32[]{:S(2)}) async-start(bf16[8,4,1792]{2,1,0:T(4,128)(2,1)} %convert_element_type.53), calls=%async_computation.2 | async-start | bytes 229376 | tf_op jit(solution)/shard_map/all_to_all | solution.py:72
Sparse Core Ops, SparseCore 0:
  10.2 55.0 all-gather.1
  96.1 19.1 reduce-scatter.1
